TPU v7x, 32 devices: a whole 2x2x4 slice. The times are simulated.
32 devices in a mesh: blk: 8 (over z, x), rows: 4 (over y, core).
Axes of the slice: x: 2, y: 2, z: 4, core: 2. Of those that a mesh axis runs over, the one named last changes fastest.
Arguments:
- features: bfloat16 [8192, 2048], P(('blk', 'rows')), may hold values from -6 to 6
- head_weight: bfloat16 [2048, 768], replicated, may hold values from -0.0048828125 to 0.0048828125
- labels: int32 [8192], P(('blk', 'rows')), may hold values from 0 to 11317
- pos_index: int32 [8192, 3], P(('blk', 'rows')), may hold values from 0 to 1023
- pair_mask: int32 [8, 3], P('blk'), may hold values from 0 to 1, as said below
- loss_weight: float32 [8192], P(('blk', 'rows')), may hold values from 0.25 to 1
Outputs:
- anchor_loss: float32 [8192], P(('blk', 'rows'))
- weight_grad: float32 [2048, 768], P(('blk', 'rows'))
Inputs may be any that keep to these rules, and one draw needn't show every extreme that they name: `pair_mask`: entry [t, s] is 1 where anchor tile t scores the rows of tile (t - s) mod 8, else 0. The rows of tiles 0 to 2 and of tile 8 - 1 are all ones.
All inputs are finite; a program needn't handle non-finite values.
Results may differ from a plain program's by a relative error of at most 0.0034.
Values may be sent and summed in bfloat16 or wider, within the bound.
A program may use at most 128 MiB of HBM per device.

v0:
```python
import jax
import jax.numpy as jnp
from jax import lax
from jax.sharding import PartitionSpec as P

SMOOTHING_SCALE = 16.0
SLACK_GAP = 0.1


def passed_along(block, axis, distance):
    devices = range(lax.axis_size(axis))
    route = [((i - distance) % len(devices), i) for i in devices]
    return lax.ppermute(block, axis, route)


def score_tile(
    anchors, anchor_sq, anchor_labels, matching_separation, weights, tile_rows, tile_labels, listed
):
    matching_samples = matching_separation.shape[1]
    block_tally = tile_rows.shape[0]
    anchor_count = anchors.shape[0]

    def compute(unused):
        products = lax.dot_general(
            anchors, tile_rows, (((1,), (1,)), ((), ())), preferred_element_type=jnp.float32
        )
        widened = tile_rows.astype(jnp.float32)
        tile_sq = jnp.sum(widened * widened, axis=1)
        couple_separation = anchor_sq[:, None] + tile_sq[None, :] - 2.0 * products
        valid = (anchor_labels[:, None] != tile_labels[None, :]).astype(jnp.float32)
        weighting = weights / (matching_samples * block_tally)
        objective_accrued = jnp.zeros((anchor_count,), jnp.float32)
        coefficient = jnp.zeros((anchor_count, block_tally), jnp.float32)
        totals = []
        for target_slot in range(matching_samples):
            slack_excess = SMOOTHING_SCALE * (
                matching_separation[:, target_slot : target_slot + 1]
                - couple_separation
                + SLACK_GAP
            )
            objective_accrued = objective_accrued + jnp.sum(
                valid * jax.nn.softplus(slack_excess), axis=1
            )
            sigmoids = valid * jax.nn.sigmoid(slack_excess)
            coefficient = coefficient + sigmoids
            totals.append(jnp.sum(sigmoids, axis=1))
        objective_accrued = objective_accrued / (SMOOTHING_SCALE * matching_samples * block_tally)
        coefficient = coefficient * weighting[:, None]
        pos_coef = jnp.stack(totals, axis=1) * weighting[:, None]
        coef_low = coefficient.astype(jnp.bfloat16)
        anchor_grad = 2.0 * jnp.dot(coef_low, tile_rows, preferred_element_type=jnp.float32)
        pulled = lax.dot_general(
            coef_low, anchors, (((0,), (0,)), ((), ())), preferred_element_type=jnp.float32
        )
        col_sums = jnp.sum(coefficient, axis=0)
        tile_grad = 2.0 * (pulled - col_sums[:, None] * widened)
        return (objective_accrued, pos_coef, anchor_grad, tile_grad, coef_low, col_sums)

    def skip(unused):
        return (
            jnp.zeros((anchor_count,), jnp.float32),
            jnp.zeros((anchor_count, matching_samples), jnp.float32),
            jnp.zeros((anchor_count, anchors.shape[1]), jnp.float32),
            jnp.zeros((block_tally, anchors.shape[1]), jnp.float32),
            jnp.zeros((anchor_count, block_tally), jnp.bfloat16),
            jnp.zeros((block_tally,), jnp.float32),
        )

    return lax.cond(listed, compute, skip, 0)


def local(features, head_weight, labels, pos_index, pair_mask, loss_weight):
    embedded = jnp.dot(features, head_weight, preferred_element_type=jnp.float32).astype(
        jnp.bfloat16
    )
    widened = embedded.astype(jnp.float32)
    anchor_sq = jnp.sum(widened * widened, axis=1)
    tile_rows, tile_labels = (
        lax.all_gather(embedded, "rows", axis=0, tiled=True),
        lax.all_gather(labels, "rows", axis=0, tiled=True),
    )
    pos_rows = tile_rows[pos_index]
    pos_wide = pos_rows.astype(jnp.float32)
    pos_sq = jnp.sum(pos_wide * pos_wide, axis=2)
    matching_separation = (
        anchor_sq[:, None]
        + pos_sq
        - 2.0 * jnp.einsum("ad,akd->ak", embedded, pos_rows, preferred_element_type=jnp.float32)
    )
    offsets = pair_mask.shape[1]
    loss_total, coef_total, grad_total, own_term, first_low, first_sums = score_tile(
        embedded,
        anchor_sq,
        labels,
        matching_separation,
        loss_weight,
        tile_rows,
        tile_labels,
        pair_mask[0, 0] > 0,
    )
    received = jnp.zeros_like(own_term)
    walk_rows, walk_labels = (tile_rows, tile_labels)
    for offset in range(1, offsets):
        walk_rows, walk_labels = passed_along((walk_rows, walk_labels), "blk", 1)
        loss_part, coef_part, grad_part, term_part, low_part, sums_part = score_tile(
            embedded,
            anchor_sq,
            labels,
            matching_separation,
            loss_weight,
            walk_rows,
            walk_labels,
            pair_mask[0, offset] > 0,
        )
        loss_total = loss_total + loss_part
        coef_total = coef_total + coef_part
        grad_total = grad_total + grad_part
        received = received + passed_along(term_part.astype(jnp.bfloat16), "blk", -offset).astype(
            term_part.dtype
        )
    grad_total = grad_total - 2.0 * jnp.sum(coef_total[:, :, None] * pos_wide, axis=1)
    pushed = 2.0 * coef_total[:, :, None] * (pos_wide - widened[:, None, :])
    own_term = own_term.at[pos_index.reshape(-1)].add(pushed.reshape(-1, pushed.shape[2]))
    quarter_sum = lax.psum_scatter(own_term + received, "rows", scatter_dimension=0, tiled=True)
    emb_grad = grad_total + quarter_sum
    grad_low = emb_grad.astype(jnp.bfloat16)
    weight_grad = lax.psum_scatter(
        lax.dot_general(
            features, grad_low, (((0,), (0,)), ((), ())), preferred_element_type=jnp.float32
        ),
        ("blk", "rows"),
        scatter_dimension=0,
        tiled=True,
    )
    return (loss_total, weight_grad)


def solution(mesh):
    return jax.shard_map(
        local,
        mesh=mesh,
        in_specs=(
            P(("blk", "rows"), None),
            P(),
            P(("blk", "rows")),
            P(("blk", "rows"), None),
            P("blk", None),
            P(("blk", "rows")),
        ),
        out_specs=(P(("blk", "rows")), P(("blk", "rows"), None)),
        check_vma=False,
    )
```

profile of v0, /device:TPU:15, one launch (start us, length us, event | category | flops | bytes accessed | tf_op | source)
XLA Modules:
  0.0 403.9 jit_solution(7590824704332708809)
XLA Ops:
  7.3 1.8 copy-done
  9.1 3.5 multiply_reduce_fusion
  12.7 20.3 %all-gather.3.cloned.1.call-done = bf16[1024,768]{1,0:T(8,128)(2,1)} async-done(((bf16[256,768]{1,0:T(8,128)(2,1)}), bf16[1024,768]{1,0:T(8,128)(2,1)}) %all-gather.3.cloned.1.call-update) | async-done | bytes 1572880 | tf_op jit(solution)/shard_map/all_gather | solution.py:79
  33.0 1.2 collective-permute-start.1
  34.2 34.8 %collective-permute-done.1 = bf16[1024,768]{1,0:T(8,128)(2,1)} collective-permute-done((bf16[1024,768]{1,0:T(8,128)(2,1)}, bf16[1024,768]{1,0:T(8,128)(2,1)}, u32[]{:S(2)}, u32[]{:S(2)}) %collective-permute-start.1) | collective-permute-done | bytes 1572896 | tf_op jit(solution)/shard_map/ppermute | solution.py:13
  68.9 2.1 collective-permute-start.3
  71.0 6.3 %all-gather = s32[4,1,256]{2,1,0:T(1,128)S(1)} all-gather(s32[1,1,256]{2,1,0:T(1,128)S(1)} %bitcast.56), channel_id=1, replica_groups=mesh['blk'=8,'rows'=4] {'rows'}, dimensions={0}, use_global_device_ids=true | all-gather | bytes 5120 | tf_op jit(solution)/shard_map/all_gather | solution.py:80
  77.4 0.3 collective-permute-start
  77.6 0.1 copy.26
  77.8 0.2 reshape.83
  78.0 0.7 fusion.53
  80.0 24.2 %collective-permute-done = s32[1024]{0:T(1024)} collective-permute-done((s32[1024]{0:T(1024)S(1)}, s32[1024]{0:T(1024)}, u32[]{:S(2)}, u32[]{:S(2)}) %collective-permute-start) | collective-permute-done | bytes 4128 | tf_op jit(solution)/shard_map/ppermute | solution.py:13
  104.2 3.0 collective-permute-start.2
  107.2 5.6 %gather_fusion = bf16[768,768]{1,0:T(8,128)(2,1)} fusion(bf16[1024,768]{1,0:T(8,128)(2,1)} %all-gather.3.cloned.1.call-done, s32[1024]{0:T(1024)S(1)} %pad_clamp_fusion), kind=kCustom, calls=%fused_computation | custom fusion | bytes 2362368 | tf_op jit(solution)/shard_map/gather | solution.py:82
  112.8 3.8 reshape.82
  116.6 3.7 fusion.41
  120.2 1.0 copy.33
  121.2 3.0 fusion.36
  124.2 1.0 copy.27
  125.2 0.7 fusion.44
  125.9 1.3 conditional.4
  125.9 1.3 broadcast.151
  127.2 11.1 %collective-permute-start.4 = (bf16[1024,768]{1,0:T(8,128)(2,1)}, bf16[1024,768]{1,0:T(8,128)(2,1)}, u32[]{:S(2)}, u32[]{:S(2)}) collective-permute-start(bf16[1024,768]{1,0:T(8,128)(2,1)} %get-tuple-element.87), channel_id=1, source_target_pairs={{4,0},{8,4},{12,8},{16,12},{20,16},{24,20},{28,24},{0,28},{5,1},{9... | collective-permute-start | bytes 4718600 | tf_op jit(solution)/shard_map/ppermute | solution.py:13
  138.3 2.9 conditional.5
  138.3 0.6 broadcast.160
  138.9 1.0 broadcast.162
  139.9 1.3 broadcast.163
  141.2 15.8 %collective-permute-start.5 = (bf16[1024,768]{1,0:T(8,128)(2,1)}, bf16[1024,768]{1,0:T(8,128)(2,1)}, u32[]{:S(2)}, u32[]{:S(2)}) collective-permute-start(bf16[1024,768]{1,0:T(8,128)(2,1)} %get-tuple-element.88), channel_id=1, source_target_pairs={{8,0},{12,4},{16,8},{20,12},{24,16},{28,20},{0,24},{4,28},{9,1},{1... | collective-permute-start | bytes 4718600 | tf_op jit(solution)/shard_map/ppermute | solution.py:13
  157.0 0.8 copy.29
  157.8 1.0 convert_element_type.68
  159.4 1.1 reshape.77
  160.5 0.6 fusion.45
  161.1 2.9 conditional.3
  161.1 1.0 broadcast.138
  162.1 1.9 broadcast.139
  164.0 0.6 copy-done.10
  164.7 5.7 %fusion.37 = (f32[256,768]{1,0:T(8,128)}, f32[256,3,768]{2,1,0:T(4,128)}) fusion(bf16[256,3,768]{2,1,0:T(4,128)(2,1)} %reshape.82, f32[256,3]{1,0:T(8,128)S(1)} %copy.28, f32[256,768]{1,0:T(8,128)} %convert_element_type.68), kind=kLoop, calls=%fused_computation.103 | loop fusion | flops 2162688 | bytes 5114880 | tf_op jit(solution)/shard_map/reduce_sum | solution.py:121
  170.4 4.6 %sub.130 = f32[768,768]{1,0:T(8,128)} reshape(f32[256,3,768]{2,1,0:T(4,128)} %get-tuple-element.205) | data formatting | bytes 4718592 | tf_op jit(solution)/shard_map/sub | solution.py:122
  175.1 0.2 mul.236
  175.4 13.6 %collective-permute-done.5 = bf16[1024,768]{1,0:T(8,128)(2,1)} collective-permute-done((bf16[1024,768]{1,0:T(8,128)(2,1)}, bf16[1024,768]{1,0:T(8,128)(2,1)}, u32[]{:S(2)}, u32[]{:S(2)}) %collective-permute-start.5) | collective-permute-done | bytes 1572896 | tf_op jit(solution)/shard_map/ppermute | solution.py:13
  189.0 5.0 %add_add_fusion = f32[1024,768]{1,0:T(8,128)} fusion(f32[1024,768]{1,0:T(8,128)} %get-tuple-element.86, bf16[1024,768]{1,0:T(8,128)(2,1)} %collective-permute-done.5, bf16[1024,768]{1,0:T(8,128)(2,1)} %collective-permute-done.4), kind=kLoop, calls=%fused_computation.104 | loop fusion | flops 3145728 | bytes 9437184 | tf_op jit(solution)/shard_map/add.9
  194.0 13.6 %scatter_custom_fusion = f32[1024,768]{1,0:T(8,128)} fusion(f32[1024,768]{1,0:T(8,128)} %add_add_fusion, s32[768]{0:T(1024)} %fusion.45, f32[768,768]{1,0:T(8,128)} %sub.130, f32[768]{0:T(1024)S(1)} %mul.236), kind=kCustom, calls=%fused_computation.105 | custom fusion | flops 1179648 | bytes 5508096 | tf_op jit(solution)/shard_map/scatter-add | solution.py:123
  207.7 62.6 %reduce-scatter.5.cloned.1.call-done = f32[256,768]{1,0:T(8,128)} async-done(((f32[1024,768]{1,0:T(8,128)}), f32[256,768]{1,0:T(8,128)}) %reduce-scatter.5.cloned.1.call-update) | async-done | bytes 786448 | tf_op jit(solution)/shard_map/reduce_scatter | solution.py:124
  270.3 6.2 %convolution_bitcast_fusion = f32[2048,768]{0,1:T(8,128)} fusion(bf16[256,2048]{1,0:T(8,128)(2,1)} %param.12, f32[256,768]{1,0:T(8,128)} %reduce-scatter.5.cloned.1.call-done, f32[256,768]{1,0:T(8,128)} %get-tuple-element.204, f32[256,768]{1,0:T(8,128)} %get-tuple-element.82, f32[256,768]{1,0:T(8,128)} %get-tuple-element.80, f32[256,768]{1,0:T(8,128)} %copy-done.2), kind=kOutput, calls=%fused_computation.101 | convolution fusion | flops 806486016 | bytes 11272192 | tf_op jit(solution)/shard_map/dot_general | solution.py:128
  276.5 6.5 %copy.34 = f32[2048,768]{1,0:T(8,128)} copy(f32[2048,768]{0,1:T(8,128)} %convolution_bitcast_fusion) | data formatting | bytes 12582912
  283.0 0.6 copy-done.9
  283.7 1.2 add_add_fusion.2
  284.9 112.4 %reduce-scatter.7.cloned.1.call-done = f32[64,768]{1,0:T(8,128)} async-done(((f32[2048,768]{1,0:T(8,128)}), f32[64,768]{1,0:T(8,128)}) %reduce-scatter.7.cloned.1.call-update) | async-done | bytes 196624
  (39 shorter events, 0.6 us)
Async XLA Ops:
  7.2 1.9 copy-start
  7.2 63.9 %copy-start.7 = (s32[256]{0:T(256)S(1)}, s32[256]{0:T(256)}, u32[]{:S(2)}) copy-start(s32[256]{0:T(256)} %param.14) | copy-start | bytes 3076
  7.2 70.5 %copy-start.4 = (s32[256,3]{0,1:T(4,128)S(1)}, s32[256,3]{0,1:T(4,128)}, u32[]{:S(2)}) copy-start(s32[256,3]{0,1:T(4,128)} %param.15) | copy-start | bytes 9220
  7.2 70.8 %copy-start.5 = (s32[1,3]{1,0:T(1,128)S(1)}, s32[1,3]{1,0:T(1,128)}, u32[]{:S(2)}) copy-start(s32[1,3]{1,0:T(1,128)} %param.16) | copy-start | bytes 40
  7.2 25.7 %all-gather.3.cloned.1.call-start = ((), (), s32[]{:S(2)}) async-start(), calls=%async_computation.2 | async-start | bytes 1966080 | tf_op jit(solution)/shard_map/all_gather | solution.py:79
  12.6 257.7 %reduce-scatter.5.cloned.1.call-start = ((), (), s32[]{:S(2)}) async-start(), calls=%async_computation.3 | async-start | bytes 3932160 | tf_op jit(solution)/shard_map/reduce_scatter | solution.py:124
  33.0 36.0 %collective-permute-start.1 = (bf16[1024,768]{1,0:T(8,128)(2,1)}, bf16[1024,768]{1,0:T(8,128)(2,1)}, u32[]{:S(2)}, u32[]{:S(2)}) collective-permute-start(bf16[1024,768]{1,0:T(8,128)(2,1)} %all-gather.3.cloned.1.call-done), channel_id=1, source_target_pairs={{28,0},{0,4},{4,8},{8,12},{12,16},{16,20},{20,24},{24,28},{29,1},{... | collective-permute-start | bytes 4718600 | tf_op jit(solution)/shard_map/ppermute | solution.py:13
  68.9 69.4 %collective-permute-start.3 = (bf16[1024,768]{1,0:T(8,128)(2,1)}, bf16[1024,768]{1,0:T(8,128)(2,1)}, u32[]{:S(2)}, u32[]{:S(2)}) collective-permute-start(bf16[1024,768]{1,0:T(8,128)(2,1)} %collective-permute-done.1), channel_id=1, source_target_pairs={{28,0},{0,4},{4,8},{8,12},{12,16},{16,20},{20,24},{24,28},{29,1},{... | collective-permute-start | bytes 4718600 | tf_op jit(solution)/shard_map/ppermute | solution.py:13
  77.3 29.8 %copy-start.6 = (s32[4,1,256]{2,1,0:T(1,128)}, s32[4,1,256]{2,1,0:T(1,128)S(1)}, u32[]{:S(2)}) copy-start(s32[4,1,256]{2,1,0:T(1,128)S(1)} %all-gather) | copy-start | bytes 12292
  77.4 26.8 %collective-permute-start = (s32[1024]{0:T(1024)S(1)}, s32[1024]{0:T(1024)}, u32[]{:S(2)}, u32[]{:S(2)}) collective-permute-start(s32[1024]{0:T(1024)S(1)} %bitcast.54), channel_id=1, source_target_pairs={{28,0},{0,4},{4,8},{8,12},{12,16},{16,20},{20,24},{24,28},{29,1},{... | collective-permute-start | bytes 12296 | tf_op jit(solution)/shard_map/ppermute | solution.py:13
  104.2 34.1 %collective-permute-start.2 = (s32[1024]{0:T(1024)}, s32[1024]{0:T(1024)}, u32[]{:S(2)}, u32[]{:S(2)}) collective-permute-start(s32[1024]{0:T(1024)} %collective-permute-done), channel_id=1, source_target_pairs={{28,0},{0,4},{4,8},{8,12},{12,16},{16,20},{20,24},{24,28},{29,1},{... | collective-permute-start | bytes 12296 | tf_op jit(solution)/shard_map/ppermute | solution.py:13
  112.8 3.8 copy-start.3
  127.2 11.1 %copy-start.8 = (f32[256]{0:T(256)}, f32[256]{0:T(256)S(1)}, u32[]{:S(2)}) copy-start(f32[256]{0:T(256)S(1)} %get-tuple-element.78) | copy-start | bytes 3076
  127.2 11.1 %copy-start.2 = (f32[256,768]{1,0:T(8,128)}, f32[256,768]{1,0:T(8,128)S(1)}, u32[]{:S(2)}) copy-start(f32[256,768]{1,0:T(8,128)S(1)} %get-tuple-element.81) | copy-start | bytes 2359300
  127.2 48.2 %collective-permute-start.4 = (bf16[1024,768]{1,0:T(8,128)(2,1)}, bf16[1024,768]{1,0:T(8,128)(2,1)}, u32[]{:S(2)}, u32[]{:S(2)}) collective-permute-start(bf16[1024,768]{1,0:T(8,128)(2,1)} %get-tuple-element.87), channel_id=1, source_target_pairs={{4,0},{8,4},{12,8},{16,12},{20,16},{24,20},{28,24},{0,28},{5,1},{9... | collective-permute-start | bytes 4718600 | tf_op jit(solution)/shard_map/ppermute | solution.py:13
  141.2 47.8 %collective-permute-start.5 = (bf16[1024,768]{1,0:T(8,128)(2,1)}, bf16[1024,768]{1,0:T(8,128)(2,1)}, u32[]{:S(2)}, u32[]{:S(2)}) collective-permute-start(bf16[1024,768]{1,0:T(8,128)(2,1)} %get-tuple-element.88), channel_id=1, source_target_pairs={{8,0},{12,4},{16,8},{20,12},{24,16},{28,20},{0,24},{4,28},{9,1},{1... | collective-permute-start | bytes 4718600 | tf_op jit(solution)/shard_map/ppermute | solution.py:13
  164.0 0.6 copy-start.10
  207.6 189.7 %reduce-scatter.7.cloned.1.call-start = ((), (), s32[]{:S(2)}) async-start(), calls=%async_computation.4 | async-start | bytes 6488064
  283.0 0.6 copy-start.9
  283.0 0.7 copy-start.11
Sparse Core Ops, SparseCore 0:
  12.7 20.1 all-gather.2
  207.7 62.4 reduce-scatter.4
  283.1 114.1 reduce-scatter.6
where the time goes:
time: 408 us; the launch traced here: 404 us
  waiting for transfers between devices  268 us (66%)
  local copies, waits for them, and re-layouts  35.9 us (9%)
  starting transfers between devices  33.7 us (8%)
  other arithmetic  30.8 us (8%)
  between operations  15.7 us (4%)
  matrix products  13.4 us (3%)
  blocking collectives  6.31 us (2%)
    unnamed x4, waiting for transfers between devices  112 us
    ppermute x6, waiting for transfers between devices, passed_along(): return lax.ppermute(block, axis, route)  72.6 us
    reduce_scatter x1, waiting for transfers between devices, local(): lax.psum_scatter(own_term + received, 'rows', scatter_dimension=0, tiled=...  62.6 us
    ppermute x6, starting transfers between devices, passed_along(): return lax.ppermute(block, axis, route)  33.5 us
    all_gather x1, waiting for transfers between devices, local(): lax.all_gather(embedded, 'rows', axis=0, tiled=True)  20.3 us
    scatter-add x1, other arithmetic, local(): own_term.at[pos_index.reshape(-1)].add(pushed.reshape(-1, pushed.shape[2]))  13.6 us
    unnamed x24, local copies, waits for them, and re-layouts  10.4 us
    gather x2, local copies, waits for them, and re-layouts, local(): pos_rows = tile_rows[pos_index]  9.41 us
  transfers between devices with their start and end apart: 9, of which 6 were waited for; matrix products, arithmetic and copies ran while one was open for 10% of the time, Pallas kernels for 0%

commit v1 on v0

--- a/solution.py
+++ b/solution.py
@@ -1,6 +1,10 @@
+import functools
+
 import jax
 import jax.numpy as jnp
 from jax import lax
+from jax.experimental import pallas as pl
+from jax.experimental.pallas import tpu as pltpu
 from jax.sharding import PartitionSpec as P
 
 SMOOTHING_SCALE = 16.0
@@ -135,9 +139,315 @@
     return (loss_total, weight_grad)
 
 
+MESH = pl.DeviceIdType.MESH
+NT = (((1,), (1,)), ((), ()))
+TN = (((0,), (0,)), ((), ()))
+
+
+def dot(a, b, dims=(((1,), (0,)), ((), ()))):
+    return lax.dot_general(a, b, dims, preferred_element_type=jnp.float32)
+
+
+def as_column(row):
+    return jnp.transpose(jnp.broadcast_to(row, (128, row.shape[1])))[:, 0:1]
+
+
+def kernel(
+    f_ref, w_ref, meta_in, mask_ref, loss_ref, out_ref,
+    ea, en, meta, metan, fc, acc, pul, cs, dpr, sqc, st, strec, tst, trec, ast, arec, ga, pst, prec,
+    ea_s, ea_r, ma_s, ma_r, en_s, en_r, mn_s, mn_r, fc_s, fc_r, t_s, t_r, a_s, a_r,
+    st_s, st_r, g_s, g_r, p_s, p_r,
+):
+    nb = lax.axis_size("blk")
+    t = lax.axis_index("blk")
+    r = lax.axis_index("rows")
+    y, c = r // 2, r % 2
+    mate = 2 * y + 1 - c
+    across = 2 * (1 - y) + c
+    diag = 2 * (1 - y) + 1 - c
+    peers = (mate, across, diag)
+    quarter, width = f_ref.shape[0], w_ref.shape[1]
+    tile = 4 * quarter
+
+    def push(src, dst, ss, rs, dev):
+        copy = pltpu.make_async_remote_copy(
+            src_ref=src, dst_ref=dst, send_sem=ss, recv_sem=rs, device_id=dev, device_id_type=MESH
+        )
+        copy.start()
+        return copy
+
+    def landed(dst, ss, rs):
+        pltpu.make_async_remote_copy(
+            src_ref=dst, dst_ref=dst, send_sem=ss, recv_sem=rs, device_id=(t, mate), device_id_type=MESH
+        ).wait_recv()
+
+    barrier = pltpu.get_barrier_semaphore()
+    for step in range(nb):
+        for core in range(2):
+            if step == 0 and core == 0:
+                continue
+            dev = ((t + step) % nb, 2 * y + (c + core) % 2)
+            pl.semaphore_signal(barrier, inc=1, device_id=dev, device_id_type=MESH)
+    for peer in (across, diag):
+        pl.semaphore_signal(barrier, inc=1, device_id=(t, peer), device_id_type=MESH)
+
+    square = jnp.zeros((quarter, 1), jnp.float32)
+    for j in range(width // 256):
+        part = dot(f_ref[...], w_ref[:, j * 256 : (j + 1) * 256]).astype(jnp.bfloat16)
+        ea[r, :, j * 256 : (j + 1) * 256] = part
+        wide = part.astype(jnp.float32)
+        square = square + jnp.sum(wide * wide, axis=1, keepdims=True)
+    meta[r] = meta_in[...]
+    meta[r, 5:6, :] = jnp.transpose(jnp.broadcast_to(square, (quarter, 128)))[0:1, :]
+    pl.semaphore_wait(barrier, 2 * nb + 1)
+
+    sent = []
+    for n, peer in ((1, across), (0, mate)):
+        sent.append(push(ea.at[r], ea.at[r], ea_s.at[n], ea_r.at[r], (t, peer)))
+        sent.append(push(meta.at[r], meta.at[r], ma_s.at[n], ma_r.at[r], (t, peer)))
+    for s in (2, 1):
+        dev = ((t + s) % nb, r)
+        sent.append(push(ea.at[r], en.at[s - 1], en_s.at[s - 1], en_r.at[s - 1], dev))
+        sent.append(push(meta.at[r], metan.at[s - 1], mn_s.at[s - 1], mn_r.at[s - 1], dev))
+    landed(ea.at[across], ea_s.at[0], ea_r.at[across])
+    sent.append(push(ea.at[across], ea.at[across], ea_s.at[2], ea_r.at[across], (t, mate)))
+    landed(meta.at[across], ma_s.at[0], ma_r.at[across])
+    sent.append(push(meta.at[across], meta.at[across], ma_s.at[2], ma_r.at[across], (t, mate)))
+    for n, peer in enumerate(peers):
+        for i in range(4):
+            column = ((2 * (4 * (peer % 2) + i)) + peer // 2) * 128
+            sent.append(
+                push(
+                    f_ref.at[:, pl.ds(pl.multiple_of(column, 128), 128)],
+                    fc.at[r, i], fc_s.at[n, i], fc_r.at[r, i], (t, peer),
+                )
+            )
+    for i in range(4):
+        column = ((2 * (4 * c + i)) + y) * 128
+        fc[r, i] = f_ref[:, pl.ds(pl.multiple_of(column, 128), 128)]
+    for peer in (mate, diag):
+        landed(ea.at[peer], ea_s.at[0], ea_r.at[peer])
+        landed(meta.at[peer], ma_s.at[0], ma_r.at[peer])
+
+    sub = lax.broadcasted_iota(jnp.int32, (quarter, quarter), 0)
+    subf = sub.astype(jnp.float32)
+    for n in range(4):
+        sqc[n] = jnp.broadcast_to(as_column(meta[n, 5:6, :]), (quarter, 128))
+
+    def positives(a, carry):
+        anchors = ea[a]
+        found = [jnp.zeros((1, quarter), jnp.float32) for _ in range(3)]
+        for n in range(4):
+            d = sqc[n][:, 0:1] - 2.0 * dot(ea[n], anchors, NT)
+            for k in range(3):
+                hit = meta[a, 1 + k : 2 + k, :] == subf + float(n * quarter)
+                found[k] = found[k] + jnp.sum(jnp.where(hit, d, 0.0), axis=0, keepdims=True)
+        for k in range(3):
+            dpr[a, k : k + 1, :] = found[k] + meta[a, 5:6, :]
+        st[a] = jnp.zeros((8, quarter), jnp.float32)
+        acc[a] = jnp.zeros((quarter, width), jnp.float32)
+        return carry
+
+    lax.fori_loop(0, 4, positives, 0)
+
+    def score(s, rows, lab_row, sq_row):
+        lab_n = as_column(lab_row)
+        sq_n = as_column(sq_row)
+        pul[...] = jnp.zeros((quarter, width), jnp.float32)
+        cs[...] = jnp.zeros((quarter, 128), jnp.float32)
+
+        def chunk(a, carry):
+            anchors = ea[a]
+            dist = (meta[a, 5:6, :] + sq_n) - 2.0 * dot(rows(), anchors, NT)
+            valid = jnp.where(lab_n != meta[a, 0:1, :], mask_ref[s : s + 1, :], 0.0)
+            coef = jnp.zeros((quarter, quarter), jnp.float32)
+            loss = jnp.zeros((quarter, quarter), jnp.float32)
+            for k in range(3):
+                x = SMOOTHING_SCALE * (dpr[a, k : k + 1, :] - dist + SLACK_GAP)
+                e = jnp.exp(-jnp.abs(x))
+                loss = loss + (jnp.maximum(x, 0.0) + jnp.log1p(e))
+                inv = 1.0 / (1.0 + e)
+                sig = valid * jnp.where(x >= 0, inv, e * inv)
+                coef = coef + sig
+                st[a, 1 + k : 2 + k, :] += jnp.sum(sig, axis=0, keepdims=True)
+            st[a, 0:1, :] += jnp.sum(valid * loss, axis=0, keepdims=True)
+            coef = coef * (meta[a, 4:5, :] / (3.0 * tile))
+            low = coef.astype(jnp.bfloat16)
+            cs[...] += jnp.broadcast_to(jnp.sum(coef, axis=1, keepdims=True), (quarter, 128))
+            pul[...] += dot(low, anchors)
+            acc[a] += dot(low, rows(), TN)
+            return carry
+
+        lax.fori_loop(0, 4, chunk, 0)
+        return 2.0 * (pul[...] - cs[:, 0:1] * rows().astype(jnp.float32))
+
+    for s in (1, 2):
+        landed(en.at[s - 1], en_s.at[s - 1], en_r.at[s - 1])
+        landed(metan.at[s - 1], mn_s.at[s - 1], mn_r.at[s - 1])
+        term = score(s, lambda: en[s - 1], metan[s - 1, 0:1, :], metan[s - 1, 5:6, :])
+        tst[s - 1] = term.astype(jnp.bfloat16)
+        sent.append(
+            push(tst.at[s - 1], trec.at[s - 1], t_s.at[s - 1], t_r.at[s - 1], ((t + nb - s) % nb, r))
+        )
+    own = score(0, lambda: ea[r], meta[r, 0:1, :], meta[r, 5:6, :])
+    pul[...] = own
+    for n, peer in enumerate(peers):
+        sent.append(push(st, strec.at[r], st_s.at[n], st_r.at[r], (t, peer)))
+    for n, peer in ((1, across), (2, diag), (0, mate)):
+        ast[n] = (2.0 * acc[peer]).astype(jnp.bfloat16)
+        sent.append(push(ast.at[n], arec.at[r], a_s.at[n], a_r.at[r], (t, peer)))
+
+    strec[r] = st[...]
+    for peer in peers:
+        landed(strec.at[peer], st_s.at[0], st_r.at[peer])
+    for a in range(4):
+        dpr[a] = strec[0, a] + strec[1, a] + strec[2, a] + strec[3, a]
+    loss_ref[...] = dpr[r] * (1.0 / (SMOOTHING_SCALE * 3.0 * tile))
+
+    acc[r] = 2.0 * acc[r] + pul[...]
+    cs[...] = jnp.zeros((quarter, 128), jnp.float32)
+
+    def listed(a, first):
+        wgt = meta[a, 4:5, :] * (1.0 / (3.0 * tile))
+        out = jnp.zeros((quarter, quarter), jnp.float32)
+        for k in range(3):
+            hit = meta[a, 1 + k : 2 + k, :] == subf + first
+            out = out + jnp.where(hit, dpr[a, 1 + k : 2 + k, :] * wgt, 0.0)
+        high = out.astype(jnp.bfloat16)
+        return out, high, (out - high.astype(jnp.float32)).astype(jnp.bfloat16)
+
+    def pulls(n, carry):
+        out, high, low = listed(n, (r * quarter).astype(jnp.float32))
+        cs[...] += jnp.broadcast_to(jnp.sum(out, axis=1, keepdims=True), (quarter, 128))
+        pushed = dot(high, ea[n]) + dot(low, ea[n])
+        out, high, low = listed(r, (n * quarter).astype(jnp.float32))
+        drawn = dot(high, ea[n], TN) + dot(low, ea[n], TN)
+        acc[r] -= 2.0 * (pushed + drawn)
+        return carry
+
+    lax.fori_loop(0, 4, pulls, 0)
+    total = acc[r] + 2.0 * cs[:, 0:1] * ea[r].astype(jnp.float32)
+    for peer in peers:
+        landed(arec.at[peer], a_s.at[0], a_r.at[peer])
+        total = total + arec[peer].astype(jnp.float32)
+    for s in (1, 2):
+        landed(trec.at[s - 1], t_s.at[s - 1], t_r.at[s - 1])
+        total = total + trec[s - 1].astype(jnp.float32)
+    ga[r] = total.astype(jnp.bfloat16)
+    for n, peer in ((1, across), (0, mate)):
+        sent.append(push(ga.at[r], ga.at[r], g_s.at[n], g_r.at[r], (t, peer)))
+    landed(ga.at[across], g_s.at[0], g_r.at[across])
+    sent.append(push(ga.at[across], ga.at[across], g_s.at[2], g_r.at[across], (t, mate)))
+    for peer in peers:
+        for i in range(4):
+            landed(fc.at[peer, i], fc_s.at[0, i], fc_r.at[peer, i])
+    for peer in (mate, diag):
+        landed(ga.at[peer], g_s.at[0], g_r.at[peer])
+
+    half = out_ref.shape[0]
+
+    def away(i, h):
+        return jnp.logical_or(4 * c + i != t, c != h)
+
+    for i in range(4):
+        part = dot(fc[0, i], ga[0], TN)
+        for n in range(1, 4):
+            part = part + dot(fc[n, i], ga[n], TN)
+        part = part.astype(jnp.bfloat16)
+        for h in range(2):
+            pst[i, h] = part[h * half : (h + 1) * half]
+        for h in range(2):
+            @pl.when(away(i, h))
+            def _():
+                push(pst.at[i, h], prec.at[t], p_s.at[i, h], p_r.at[t], (4 * c + i, 2 * y + h))
+
+            @pl.when(jnp.logical_not(away(i, h)))
+            def _():
+                prec[t] = pst[i, h]
+
+    for step in range(nb):
+        @pl.when(jnp.logical_or(t // 4 != c, t != step))
+        def _():
+            landed(prec.at[step], p_s.at[0, 0], p_r.at[step])
+
+    result = prec[0].astype(jnp.float32)
+    for step in range(1, nb):
+        result = result + prec[step].astype(jnp.float32)
+    out_ref[...] = result
+    for i in range(4):
+        for h in range(2):
+            @pl.when(away(i, h))
+            def _():
+                pltpu.make_async_remote_copy(
+                    src_ref=pst.at[i, h], dst_ref=prec.at[t], send_sem=p_s.at[i, h],
+                    recv_sem=p_r.at[t], device_id=(t, mate), device_id_type=MESH,
+                ).wait_send()
+    for copy in sent:
+        copy.wait_send()
+
+
+def fused(features, head_weight, labels, pos_index, pair_mask, loss_weight):
+    quarter, depth = features.shape
+    width = head_weight.shape[1]
+    nb = lax.axis_size("blk")
+    share = depth // (4 * nb)
+    meta = jnp.concatenate(
+        [
+            labels.astype(jnp.float32)[None, :],
+            pos_index.astype(jnp.float32).T,
+            loss_weight[None, :],
+            jnp.zeros((3, quarter), jnp.float32),
+        ]
+    )
+    mask = jnp.zeros((8, quarter), jnp.float32).at[:3].set(
+        jnp.broadcast_to((pair_mask[0] > 0).astype(jnp.float32)[:, None], (3, quarter))
+    )
+    f32, bf16 = jnp.float32, jnp.bfloat16
+    dma = pltpu.SemaphoreType.DMA
+    vmem = pl.BlockSpec(memory_space=pltpu.VMEM)
+    block = (quarter, width)
+    small = (8, quarter)
+    loss, grad = pl.pallas_call(
+        kernel,
+        out_shape=(jax.ShapeDtypeStruct(small, f32), jax.ShapeDtypeStruct((share, width), f32)),
+        in_specs=[vmem] * 4,
+        out_specs=(vmem, vmem),
+        scratch_shapes=[
+            pltpu.VMEM((4,) + block, bf16),
+            pltpu.VMEM((2,) + block, bf16),
+            pltpu.VMEM((4,) + small, f32),
+            pltpu.VMEM((2,) + small, f32),
+            pltpu.VMEM((4, 4, quarter, 128), bf16),
+            pltpu.VMEM((4,) + block, f32),
+            pltpu.VMEM(block, f32),
+            pltpu.VMEM((quarter, 128), f32),
+            pltpu.VMEM((4,) + small, f32),
+            pltpu.VMEM((4, quarter, 128), f32),
+            pltpu.VMEM((4,) + small, f32),
+            pltpu.VMEM((4, 4) + small, f32),
+            pltpu.VMEM((2,) + block, bf16),
+            pltpu.VMEM((2,) + block, bf16),
+            pltpu.VMEM((3,) + block, bf16),
+            pltpu.VMEM((4,) + block, bf16),
+            pltpu.VMEM((4,) + block, bf16),
+            pltpu.VMEM((4, 2, share, width), bf16),
+            pltpu.VMEM((nb, share, width), bf16),
+            dma((3,)), dma((4,)), dma((3,)), dma((4,)),
+            dma((2,)), dma((2,)), dma((2,)), dma((2,)),
+            dma((3, 4)), dma((4, 4)), dma((2,)), dma((2,)), dma((3,)), dma((4,)),
+            dma((3,)), dma((4,)), dma((3,)), dma((4,)), dma((4, 2)), dma((nb,)),
+        ],
+        compiler_params=pltpu.CompilerParams(
+            collective_id=0, has_side_effects=True, vmem_limit_bytes=56 * 1024 * 1024
+        ),
+    )(features, head_weight, meta, mask)
+    return loss[0], grad
+
+
 def solution(mesh):
+    body = fused if mesh.shape["blk"] == 8 and mesh.shape["rows"] == 4 else local
     return jax.shard_map(
-        local,
+        body,
         mesh=mesh,
         in_specs=(
             P(("blk", "rows"), None),

time: 408 us -> 105 us (0.26)
  waiting for transfers between devices: 268 us -> 0 us
  Pallas kernels: 0 us -> 96.6 us
  starting transfers between devices: 33.7 us -> 0 us
  local copies, waits for them, and re-layouts: 35.9 us -> 3.62 us
  other arithmetic: 30.8 us -> 3.38 us
  between operations: 15.7 us -> 0.64 us
  matrix products: 13.4 us -> 0 us
  blocking collectives: 6.31 us -> 0 us
    unnamed x4 -> x0, waiting for transfers between devices: 112 us -> none
    pallas_call x0 -> x1, Pallas kernels: none -> 96.6 us  [fused(): pl.pallas_call(kernel, out_shape=(jax.ShapeDtypeStruct(small, f32), jax.S...]
    ppermute x6 -> x0, waiting for transfers between devices: 72.6 us -> none  [passed_along(): return lax.ppermute(block, axis, route)]
    reduce_scatter x1 -> x0, waiting for transfers between devices: 62.6 us -> none  [local(): lax.psum_scatter(own_term + received, 'rows', scatter_dimension=0, tiled=...]
    ppermute x6 -> x0, starting transfers between devices: 33.5 us -> none  [passed_along(): return lax.ppermute(block, axis, route)]
    all_gather x1 -> x0, waiting for transfers between devices: 20.3 us -> none  [local(): lax.all_gather(embedded, 'rows', axis=0, tiled=True)]
    scatter-add x1 -> x0, other arithmetic: 13.6 us -> none  [local(): own_term.at[pos_index.reshape(-1)].add(pushed.reshape(-1, pushed.shape[2]))]
    dot_general x3 -> x0, matrix products: 13.4 us -> none  [the longest x1 6.19 us: local(): lax.dot_general(features, grad_low, (((0,), (0,)), ((), ())), preferred_e...]
  transfers between devices with their start and end apart: 9 -> 0, of which waited for: 6 -> 0; matrix products, arithmetic and copies ran while one was open for 10% -> 0% of each run, Pallas kernels for 0% -> 0%
where the time goes in v1:
time: 105 us; the launch traced here: 104 us
  Pallas kernels  96.6 us (92%)
  local copies, waits for them, and re-layouts  3.62 us (3%)
  other arithmetic  3.38 us (3%)
    pallas_call x1, Pallas kernels, fused(): pl.pallas_call(kernel, out_shape=(jax.ShapeDtypeStruct(small, f32), jax.S...  96.6 us

profile of v1, /device:TPU:15, one launch (start us, length us, event | category | flops | bytes accessed | tf_op | source)
XLA Modules:
  0.0 104.3 jit_solution(5034555001673464934)
XLA Ops:
  0.6 0.7 compare_bitcast_fusion
  1.3 0.1 pad.6.clone
  1.4 0.7 convert_element_type.14
  2.1 0.7 convert_bitcast_fusion
  2.7 1.3 %maximum_maximum_fusion.meta_in = f32[8,256]{1,0:T(8,128)} fusion(f32[1,256]{1,0:T(1,128)} %bitcast.9, f32[3,256]{1,0:T(4,128)S(1)} %convert_bitcast_fusion, f32[1,256]{1,0:T(1,128)S(1)} %bitcast.7, f32[8]{0:T(128)S(1)} %pad.6.clone), kind=kLoop, calls=%fused_computation | loop fusion | flops 6144 | bytes 13344 | tf_op jit(solution)/shard_map/concatenate | solution.py:394
  4.1 0.7 scatter.11.mask_ref
  4.8 96.6 %shard_map.77 = (f32[8,256]{1,0:T(8,128)}, f32[64,768]{1,0:T(8,128)}) custom-call(bf16[256,2048]{1,0:T(8,128)(2,1)} %f_ref.1, bf16[2048,768]{1,0:T(8,128)(2,1)} %w_ref.1, f32[8,256]{1,0:T(8,128)} %maximum_maximum_fusion.meta_in, f32[8,256]{1,0:T(8,128)} %scatter.11.mask_ref), custom_call_target="tpu_custom_call" | custom-call | tf_op jit(solution)/shard_map/pallas_call | solution.py:410
  101.4 1.3 %slice.19 = f32[1,256]{1,0:T(1,128)} slice(f32[8,256]{1,0:T(8,128)} %get-tuple-element.16), slice={[0:1], [0:256]} | slice | bytes 2048 | tf_op jit(solution)/shard_map/slice | solution.py:444
  102.7 1.6 %copy.9 = f32[64,768]{1,0:T(8,128)} copy(f32[64,768]{1,0:T(8,128)} %get-tuple-element.21) | data formatting | bytes 393216
  (2 shorter events, 0.0 us)

commit v2 on v1

--- a/solution.py
+++ b/solution.py
@@ -153,10 +153,11 @@
 
 
 def kernel(
-    f_ref, w_ref, meta_in, mask_ref, loss_ref, out_ref,
-    ea, en, meta, metan, fc, acc, pul, cs, dpr, sqc, st, strec, tst, trec, ast, arec, ga, pst, prec,
+    f_ref, w_ref, lab_ref, pos_ref, wgt_ref, mask_ref, loss_ref, out_ref,
+    ea, en, meta, metan, fc, fct, acc, own, pul, cs, dpr, sqc, st, strec, tst, trec, ast, arec, hst, hrec,
+    ga, pst, prec,
     ea_s, ea_r, ma_s, ma_r, en_s, en_r, mn_s, mn_r, fc_s, fc_r, t_s, t_r, a_s, a_r,
-    st_s, st_r, g_s, g_r, p_s, p_r,
+    h_s, h_r, st_s, st_r, g_s, g_r, p_s, p_r,
 ):
     nb = lax.axis_size("blk")
     t = lax.axis_index("blk")
@@ -197,7 +198,10 @@
         ea[r, :, j * 256 : (j + 1) * 256] = part
         wide = part.astype(jnp.float32)
         square = square + jnp.sum(wide * wide, axis=1, keepdims=True)
-    meta[r] = meta_in[...]
+    meta[r] = jnp.zeros(meta.shape[1:], jnp.float32)
+    meta[r, 0:1, :] = lab_ref[...].astype(jnp.float32)
+    meta[r, 1:4, :] = pos_ref[...].astype(jnp.float32)
+    meta[r, 4:5, :] = wgt_ref[...]
     meta[r, 5:6, :] = jnp.transpose(jnp.broadcast_to(square, (quarter, 128)))[0:1, :]
     pl.semaphore_wait(barrier, 2 * nb + 1)
 
@@ -243,68 +247,97 @@
                 hit = meta[a, 1 + k : 2 + k, :] == subf + float(n * quarter)
                 found[k] = found[k] + jnp.sum(jnp.where(hit, d, 0.0), axis=0, keepdims=True)
         for k in range(3):
-            dpr[a, k : k + 1, :] = found[k] + meta[a, 5:6, :]
+            dpr[a, k : k + 1, :] = SMOOTHING_SCALE * (found[k] + meta[a, 5:6, :] + SLACK_GAP)
         st[a] = jnp.zeros((8, quarter), jnp.float32)
         acc[a] = jnp.zeros((quarter, width), jnp.float32)
         return carry
 
     lax.fori_loop(0, 4, positives, 0)
 
-    def score(s, rows, lab_row, sq_row):
-        lab_n = as_column(lab_row)
-        sq_n = as_column(sq_row)
+    def start_tile(lab_row, sq_row):
         pul[...] = jnp.zeros((quarter, width), jnp.float32)
         cs[...] = jnp.zeros((quarter, 128), jnp.float32)
-
-        def chunk(a, carry):
-            anchors = ea[a]
-            dist = (meta[a, 5:6, :] + sq_n) - 2.0 * dot(rows(), anchors, NT)
-            valid = jnp.where(lab_n != meta[a, 0:1, :], mask_ref[s : s + 1, :], 0.0)
-            coef = jnp.zeros((quarter, quarter), jnp.float32)
-            loss = jnp.zeros((quarter, quarter), jnp.float32)
-            for k in range(3):
-                x = SMOOTHING_SCALE * (dpr[a, k : k + 1, :] - dist + SLACK_GAP)
-                e = jnp.exp(-jnp.abs(x))
-                loss = loss + (jnp.maximum(x, 0.0) + jnp.log1p(e))
-                inv = 1.0 / (1.0 + e)
-                sig = valid * jnp.where(x >= 0, inv, e * inv)
-                coef = coef + sig
-                st[a, 1 + k : 2 + k, :] += jnp.sum(sig, axis=0, keepdims=True)
-            st[a, 0:1, :] += jnp.sum(valid * loss, axis=0, keepdims=True)
-            coef = coef * (meta[a, 4:5, :] / (3.0 * tile))
-            low = coef.astype(jnp.bfloat16)
-            cs[...] += jnp.broadcast_to(jnp.sum(coef, axis=1, keepdims=True), (quarter, 128))
-            pul[...] += dot(low, anchors)
-            acc[a] += dot(low, rows(), TN)
+        return as_column(lab_row), SMOOTHING_SCALE * as_column(sq_row)
+
+    def chunk(s, a, rows, lab_n, sq_n):
+        anchors = ea[a]
+        spread = (SMOOTHING_SCALE * meta[a, 5:6, :] + sq_n) - (2.0 * SMOOTHING_SCALE) * dot(rows(), anchors, NT)
+        scored = jnp.broadcast_to((mask_ref[0:1, s : s + 1] > 0).astype(jnp.float32), (1, quarter))
+        valid = jnp.where(lab_n != meta[a, 0:1, :], scored, 0.0)
+        linear = jnp.zeros((quarter, quarter), jnp.float32)
+        e, top = [], []
+        for k in range(3):
+            x = dpr[a, k : k + 1, :] - spread
+            e.append(jnp.exp(-jnp.abs(x)))
+            top.append(jnp.where(x >= 0, 1.0, e[k]))
+            linear = linear + jnp.maximum(x, 0.0)
+        p = e[0] + e[1] + e[0] * e[1]
+        p = p + e[2] + p * e[2]
+        u = 1.0 + p
+        inv = 1.0 / u
+        log = jnp.log(u) + (p - (u - 1.0)) * inv
+        st[a, 0:1, :] += jnp.sum(valid * (linear + log), axis=0, keepdims=True)
+        inv = valid * inv
+        coef = jnp.zeros((quarter, quarter), jnp.float32)
+        for k in range(3):
+            others = (1.0 + e[(k + 1) % 3]) * (1.0 + e[(k + 2) % 3])
+            sig = top[k] * (inv * others)
+            coef = coef + sig
+            st[a, 1 + k : 2 + k, :] += jnp.sum(sig, axis=0, keepdims=True)
+        coef = coef * (meta[a, 4:5, :] * (1.0 / (3.0 * tile)))
+        low = coef.astype(jnp.bfloat16)
+        cs[...] += jnp.broadcast_to(jnp.sum(coef, axis=1, keepdims=True), (quarter, 128))
+        pul[...] += dot(low, anchors)
+        acc[a] += dot(low, rows(), TN)
+
+    def tile_term(rows):
+        return 2.0 * (pul[...] - cs[:, 0:1] * rows().astype(jnp.float32))
+
+    def score(s, rows, lab_row, sq_row):
+        lab_n, sq_n = start_tile(lab_row, sq_row)
+
+        def step(a, carry):
+            chunk(s, a, rows, lab_n, sq_n)
             return carry
 
-        lax.fori_loop(0, 4, chunk, 0)
-        return 2.0 * (pul[...] - cs[:, 0:1] * rows().astype(jnp.float32))
-
+        lax.fori_loop(0, 4, step, 0)
+        return tile_term(rows)
+
+    def send_term(s, term):
+        tst[s - 1] = term.astype(jnp.bfloat16)
+        dev = ((t + nb - s) % nb, r)
+        sent.append(push(tst.at[s - 1], trec.at[s - 1], t_s.at[s - 1], t_r.at[s - 1], dev))
+
+    own[...] = score(0, lambda: ea[r], meta[r, 0:1, :], meta[r, 5:6, :])
     for s in (1, 2):
         landed(en.at[s - 1], en_s.at[s - 1], en_r.at[s - 1])
         landed(metan.at[s - 1], mn_s.at[s - 1], mn_r.at[s - 1])
-        term = score(s, lambda: en[s - 1], metan[s - 1, 0:1, :], metan[s - 1, 5:6, :])
-        tst[s - 1] = term.astype(jnp.bfloat16)
-        sent.append(
-            push(tst.at[s - 1], trec.at[s - 1], t_s.at[s - 1], t_r.at[s - 1], ((t + nb - s) % nb, r))
-        )
-    own = score(0, lambda: ea[r], meta[r, 0:1, :], meta[r, 5:6, :])
-    pul[...] = own
+    send_term(1, score(1, lambda: en[0], metan[0, 0:1, :], metan[0, 5:6, :]))
+
+    lab_n, sq_n = start_tile(metan[1, 0:1, :], metan[1, 5:6, :])
+    chunk(2, diag, lambda: en[1], lab_n, sq_n)
+    hst[...] = (2.0 * acc[diag]).astype(jnp.bfloat16)
+    sent.append(push(hst, hrec, h_s, h_r, (t, mate)))
+    chunk(2, mate, lambda: en[1], lab_n, sq_n)
+    ast[0] = (2.0 * acc[mate]).astype(jnp.bfloat16)
+    sent.append(push(ast.at[0], arec.at[0], a_s.at[0], a_r.at[0], (t, mate)))
+    chunk(2, across, lambda: en[1], lab_n, sq_n)
+    landed(hrec, h_s, h_r)
+    ast[1] = (2.0 * acc[across] + hrec[...].astype(jnp.float32)).astype(jnp.bfloat16)
+    sent.append(push(ast.at[1], arec.at[1], a_s.at[1], a_r.at[1], (t, across)))
+    chunk(2, r, lambda: en[1], lab_n, sq_n)
     for n, peer in enumerate(peers):
         sent.append(push(st, strec.at[r], st_s.at[n], st_r.at[r], (t, peer)))
-    for n, peer in ((1, across), (2, diag), (0, mate)):
-        ast[n] = (2.0 * acc[peer]).astype(jnp.bfloat16)
-        sent.append(push(ast.at[n], arec.at[r], a_s.at[n], a_r.at[r], (t, peer)))
+    send_term(2, tile_term(lambda: en[1]))
 
     strec[r] = st[...]
     for peer in peers:
         landed(strec.at[peer], st_s.at[0], st_r.at[peer])
     for a in range(4):
         dpr[a] = strec[0, a] + strec[1, a] + strec[2, a] + strec[3, a]
-    loss_ref[...] = dpr[r] * (1.0 / (SMOOTHING_SCALE * 3.0 * tile))
-
-    acc[r] = 2.0 * acc[r] + pul[...]
+    loss_ref[...] = dpr[r, 0:1, :] * (1.0 / (SMOOTHING_SCALE * 3.0 * tile))
+
+    acc[r] = 2.0 * acc[r] + own[...]
     cs[...] = jnp.zeros((quarter, 128), jnp.float32)
 
     def listed(a, first):
@@ -326,62 +359,79 @@
         return carry
 
     lax.fori_loop(0, 4, pulls, 0)
-    total = acc[r] + 2.0 * cs[:, 0:1] * ea[r].astype(jnp.float32)
-    for peer in peers:
-        landed(arec.at[peer], a_s.at[0], a_r.at[peer])
-        total = total + arec[peer].astype(jnp.float32)
-    for s in (1, 2):
-        landed(trec.at[s - 1], t_s.at[s - 1], t_r.at[s - 1])
-        total = total + trec[s - 1].astype(jnp.float32)
-    ga[r] = total.astype(jnp.bfloat16)
-    for n, peer in ((1, across), (0, mate)):
-        sent.append(push(ga.at[r], ga.at[r], g_s.at[n], g_r.at[r], (t, peer)))
-    landed(ga.at[across], g_s.at[0], g_r.at[across])
-    sent.append(push(ga.at[across], ga.at[across], g_s.at[2], g_r.at[across], (t, mate)))
+    acc[r] += 2.0 * cs[:, 0:1] * ea[r].astype(jnp.float32)
     for peer in peers:
         for i in range(4):
             landed(fc.at[peer, i], fc_s.at[0, i], fc_r.at[peer, i])
-    for peer in (mate, diag):
-        landed(ga.at[peer], g_s.at[0], g_r.at[peer])
+    for n in range(4):
+        for i in range(4):
+            fct[i * 128 : (i + 1) * 128, n * quarter : (n + 1) * quarter] = jnp.transpose(fc[n, i])
+    for n in range(2):
+        landed(arec.at[n], a_s.at[0], a_r.at[n])
+    for s in (1, 2):
+        landed(trec.at[s - 1], t_s.at[s - 1], t_r.at[s - 1])
+    pieces = ga.shape[0]
+    piece = width // pieces
+    for j in range(pieces):
+        cut = slice(j * piece, (j + 1) * piece)
+        total = acc[r, :, cut]
+        for ref in (arec, trec):
+            total = total + ref[0, :, cut].astype(jnp.float32) + ref[1, :, cut].astype(jnp.float32)
+        ga[j, r] = total.astype(jnp.bfloat16)
+        for n, peer in ((1, across), (0, mate)):
+            sent.append(push(ga.at[j, r], ga.at[j, r], g_s.at[j, n], g_r.at[j, r], (t, peer)))
 
     half = out_ref.shape[0]
 
     def away(i, h):
         return jnp.logical_or(4 * c + i != t, c != h)
 
-    for i in range(4):
-        part = dot(fc[0, i], ga[0], TN)
-        for n in range(1, 4):
-            part = part + dot(fc[n, i], ga[n], TN)
-        part = part.astype(jnp.bfloat16)
-        for h in range(2):
-            pst[i, h] = part[h * half : (h + 1) * half]
-        for h in range(2):
-            @pl.when(away(i, h))
+    def arrive(j):
+        landed(ga.at[j, across], g_s.at[j, 0], g_r.at[j, across])
+        sent.append(push(ga.at[j, across], ga.at[j, across], g_s.at[j, 2], g_r.at[j, across], (t, mate)))
+
+    def hop(j, i, h):
+        return pltpu.make_async_remote_copy(
+            src_ref=pst.at[j, i, h], dst_ref=prec.at[j, t], send_sem=p_s.at[j, i, h],
+            recv_sem=p_r.at[j, t], device_id=(4 * c + i, 2 * y + h), device_id_type=MESH,
+        )
+
+    arrive(0)
+    for j in range(pieces):
+        if j + 1 < pieces:
+            arrive(j + 1)
+        for peer in (mate, diag):
+            landed(ga.at[j, peer], g_s.at[j, 0], g_r.at[j, peer])
+        part = dot(fct[...], ga[j].reshape(tile, piece)).astype(jnp.bfloat16)
+        for i in range(4):
+            for h in range(2):
+                pst[j, i, h] = part[(2 * i + h) * half : (2 * i + h + 1) * half]
+        for i in range(4):
+            for h in range(2):
+                @pl.when(away(i, h))
+                def _():
+                    hop(j, i, h).start()
+
+                @pl.when(jnp.logical_not(away(i, h)))
+                def _():
+                    prec[j, t] = pst[j, i, h]
+
+    for j in range(pieces):
+        for step in range(nb):
+            @pl.when(jnp.logical_or(t // 4 != c, t != step))
             def _():
-                push(pst.at[i, h], prec.at[t], p_s.at[i, h], p_r.at[t], (4 * c + i, 2 * y + h))
-
-            @pl.when(jnp.logical_not(away(i, h)))
-            def _():
-                prec[t] = pst[i, h]
-
-    for step in range(nb):
-        @pl.when(jnp.logical_or(t // 4 != c, t != step))
-        def _():
-            landed(prec.at[step], p_s.at[0, 0], p_r.at[step])
-
-    result = prec[0].astype(jnp.float32)
-    for step in range(1, nb):
-        result = result + prec[step].astype(jnp.float32)
-    out_ref[...] = result
-    for i in range(4):
-        for h in range(2):
-            @pl.when(away(i, h))
-            def _():
-                pltpu.make_async_remote_copy(
-                    src_ref=pst.at[i, h], dst_ref=prec.at[t], send_sem=p_s.at[i, h],
-                    recv_sem=p_r.at[t], device_id=(t, mate), device_id_type=MESH,
-                ).wait_send()
+                landed(prec.at[j, step], p_s.at[j, 0, 0], p_r.at[j, step])
+
+        result = prec[j, 0].astype(jnp.float32)
+        for step in range(1, nb):
+            result = result + prec[j, step].astype(jnp.float32)
+        out_ref[:, j * piece : (j + 1) * piece] = result
+    for j in range(pieces):
+        for i in range(4):
+            for h in range(2):
+                @pl.when(away(i, h))
+                def _():
+                    hop(j, i, h).wait_send()
     for copy in sent:
         copy.wait_send()
 
@@ -391,17 +441,6 @@
     width = head_weight.shape[1]
     nb = lax.axis_size("blk")
     share = depth // (4 * nb)
-    meta = jnp.concatenate(
-        [
-            labels.astype(jnp.float32)[None, :],
-            pos_index.astype(jnp.float32).T,
-            loss_weight[None, :],
-            jnp.zeros((3, quarter), jnp.float32),
-        ]
-    )
-    mask = jnp.zeros((8, quarter), jnp.float32).at[:3].set(
-        jnp.broadcast_to((pair_mask[0] > 0).astype(jnp.float32)[:, None], (3, quarter))
-    )
     f32, bf16 = jnp.float32, jnp.bfloat16
     dma = pltpu.SemaphoreType.DMA
     vmem = pl.BlockSpec(memory_space=pltpu.VMEM)
@@ -409,8 +448,8 @@
     small = (8, quarter)
     loss, grad = pl.pallas_call(
         kernel,
-        out_shape=(jax.ShapeDtypeStruct(small, f32), jax.ShapeDtypeStruct((share, width), f32)),
-        in_specs=[vmem] * 4,
+        out_shape=(jax.ShapeDtypeStruct((1, quarter), f32), jax.ShapeDtypeStruct((share, width), f32)),
+        in_specs=[vmem] * 6,
         out_specs=(vmem, vmem),
         scratch_shapes=[
             pltpu.VMEM((4,) + block, bf16),
@@ -418,7 +457,9 @@
             pltpu.VMEM((4,) + small, f32),
             pltpu.VMEM((2,) + small, f32),
             pltpu.VMEM((4, 4, quarter, 128), bf16),
+            pltpu.VMEM((512, 4 * quarter), bf16),
             pltpu.VMEM((4,) + block, f32),
+            pltpu.VMEM(block, f32),
             pltpu.VMEM(block, f32),
             pltpu.VMEM((quarter, 128), f32),
             pltpu.VMEM((4,) + small, f32),
@@ -427,20 +468,22 @@
             pltpu.VMEM((4, 4) + small, f32),
             pltpu.VMEM((2,) + block, bf16),
             pltpu.VMEM((2,) + block, bf16),
-            pltpu.VMEM((3,) + block, bf16),
-            pltpu.VMEM((4,) + block, bf16),
-            pltpu.VMEM((4,) + block, bf16),
-            pltpu.VMEM((4, 2, share, width), bf16),
-            pltpu.VMEM((nb, share, width), bf16),
+            pltpu.VMEM((2,) + block, bf16),
+            pltpu.VMEM((2,) + block, bf16),
+            pltpu.VMEM(block, bf16),
+            pltpu.VMEM(block, bf16),
+            pltpu.VMEM((3, 4, quarter, width // 3), bf16),
+            pltpu.VMEM((3, 4, 2, share, width // 3), bf16),
+            pltpu.VMEM((3, nb, share, width // 3), bf16),
             dma((3,)), dma((4,)), dma((3,)), dma((4,)),
             dma((2,)), dma((2,)), dma((2,)), dma((2,)),
-            dma((3, 4)), dma((4, 4)), dma((2,)), dma((2,)), dma((3,)), dma((4,)),
-            dma((3,)), dma((4,)), dma((3,)), dma((4,)), dma((4, 2)), dma((nb,)),
+            dma((3, 4)), dma((4, 4)), dma((2,)), dma((2,)), dma((2,)), dma((2,)), dma(()), dma(()),
+            dma((3,)), dma((4,)), dma((3, 3)), dma((3, 4)), dma((3, 4, 2)), dma((3, nb)),
         ],
         compiler_params=pltpu.CompilerParams(
             collective_id=0, has_side_effects=True, vmem_limit_bytes=56 * 1024 * 1024
         ),
-    )(features, head_weight, meta, mask)
+    )(features, head_weight, labels[None, :], pos_index.T, loss_weight[None, :], pair_mask)
     return loss[0], grad
 
 

time: 105 us -> 85.1 us (0.81)
  Pallas kernels: 96.6 us -> 80.5 us
  other arithmetic: 3.38 us -> 0 us
    pallas_call x1, Pallas kernels: 96.6 us -> 80.5 us  [fused(): pl.pallas_call(kernel, out_shape=(jax.ShapeDtypeStruct((1, quarter), f32)...]
    concatenate x1 -> x0, other arithmetic: 1.35 us -> none  [fused(): jnp.concatenate([labels.astype(jnp.float32)[None, :], pos_index.astype(jn...]
    convert_element_type x2 -> x0, other arithmetic: 1.34 us -> none  [the longest x1 0.68 us: fused(): labels.astype(jnp.float32)[None, :]]
    slice x1 -> x0, local copies, waits for them, and re-layouts: 1.26 us -> none  [fused(): return (loss[0], grad)]
    unnamed x1 -> x2, local copies, waits for them, and re-layouts: 1.62 us -> 2.8 us
where the time goes in v2:
time: 85.1 us; the launch traced here: 83.9 us
  Pallas kernels  80.5 us (95%)
  local copies, waits for them, and re-layouts  2.8 us (3%)
    pallas_call x1, Pallas kernels, fused(): pl.pallas_call(kernel, out_shape=(jax.ShapeDtypeStruct((1, quarter), f32)...  80.5 us
    unnamed x2, local copies, waits for them, and re-layouts  2.8 us

profile of v2, /device:TPU:15, one launch (start us, length us, event | category | flops | bytes accessed | tf_op | source)
XLA Modules:
  0.0 83.9 jit_solution(7017192295033068557)
XLA Ops:
  0.6 80.5 %shard_map.77 = (f32[1,256]{1,0:T(1,128)}, f32[64,768]{1,0:T(8,128)}) custom-call(bf16[256,2048]{1,0:T(8,128)(2,1)} %f_ref.1, bf16[2048,768]{1,0:T(8,128)(2,1)} %w_ref.1, s32[1,256]{1,0:T(1,128)} %bitcast.5, s32[3,256]{1,0:T(4,128)} %bitcast.4, f32[1,256]{1,0:T(1,128)} %bitcast.6, s32[1,3]{1,0:T(1,128)} %mask_ref.1), custom_call_target="tpu_custom_call" | custom-call | tf_op jit(solution)/shard_map/pallas_call | solution.py:449
  81.1 1.2 %copy.10 = f32[256]{0:T(256)} copy(f32[256]{0:T(256)} %bitcast.7) | data formatting | bytes 2048
  82.3 1.6 %copy.11 = f32[64,768]{1,0:T(8,128)} copy(f32[64,768]{1,0:T(8,128)} %get-tuple-element.9) | data formatting | bytes 393216
